TPU v7x, 32 devices: a whole 2x2x4 slice. The times are simulated.
32 devices in a mesh: src: 8 (over z, y), snk: 4 (over x, core).
Axes of the slice: x: 2, y: 2, z: 4, core: 2. Of those that a mesh axis runs over, the one named last changes fastest.
Arguments:
- tau_cols: bfloat16 [2, 8, 8, 256, 256], P(None, 'src', None, 'snk'), may hold values from -0.25 to 0.25
- elementals: bfloat16 [256, 2, 256, 256], P('src'), may hold values from -0.25 to 0.25
- need_ids: int32 [8, 8], replicated, may hold values from 0 to 255, as said below
- diagrams: int32 [8, 8, 3], P('src'), may hold values from 0 to 15, as said below
- phases: int32 [16], replicated, may hold values from 0 to 3
- block_sizes: int32 [4], replicated, may hold values from 1 to 3, 8 in all
Outputs:
- correlators: float32 [8, 4, 3, 2, 8], P('src', 'snk')
Inputs may be any that keep to these rules, and one draw needn't show every extreme that they name: `block_sizes`: the sizes sum to 8, and one of them is exactly 3. `need_ids`: the 8 ids of a row are distinct. `diagrams`: entry 0 of a diagram is below 4, entry 1 below 4, entry 2 below 16; each of a row's 4 sink-side and 4 source-side entries is named by some diagram of the row.
All inputs are finite; a program needn't handle non-finite values.
Results may differ from a plain program's by a relative error of at most 0.004.
Values may be sent and summed in bfloat16 or wider, within the bound.
A program may use at most 64 MiB of HBM per device.

v0:
```python
import jax
import jax.numpy as jnp
from jax import lax
from jax.sharding import PartitionSpec as P

NSN = 4
MAXB = 3


def slot_values(gathered, tau_slot, diagram_rows, phases):
    real_part = tau_slot[0]
    imag_part = tau_slot[1]
    left_stack = jnp.stack([jnp.stack([real_part, imag_part]), jnp.stack([-imag_part, real_part])])
    right_stack = jnp.stack([jnp.stack([real_part, -imag_part]), jnp.stack([imag_part, real_part])])
    left_node = lax.dot_general(
        gathered[:, :, :NSN],
        left_stack,
        (((1, 3), (0, 3)), ((), ())),
        preferred_element_type=jnp.float32,
    ).astype(jnp.bfloat16)
    right_node = lax.dot_general(
        gathered[:, :, NSN:],
        right_stack,
        (((1, 3), (0, 2)), ((), ())),
        preferred_element_type=jnp.float32,
    ).astype(jnp.bfloat16)
    pair_sums = lax.dot_general(
        left_node, right_node, (((0, 3), (3, 0)), ((), ())), preferred_element_type=jnp.float32
    )
    pair_real = pair_sums[:, 0, :, 0] - pair_sums[:, 1, :, 1]
    pair_imag = pair_sums[:, 0, :, 1] + pair_sums[:, 1, :, 0]
    sink_pick = (
        diagram_rows[:, 0:1] == jnp.arange(pair_real.shape[0], dtype=jnp.int32)[None, :]
    ).astype(jnp.float32)
    source_pick = (
        diagram_rows[:, 1:2] == jnp.arange(pair_real.shape[1], dtype=jnp.int32)[None, :]
    ).astype(jnp.float32)
    chosen_real = jnp.sum(
        sink_pick[:, :, None] * pair_real[None] * source_pick[:, None, :], axis=(1, 2)
    )
    chosen_imag = jnp.sum(
        sink_pick[:, :, None] * pair_imag[None] * source_pick[:, None, :], axis=(1, 2)
    )
    gamma_pick = diagram_rows[:, 2:3] == jnp.arange(phases.shape[0], dtype=jnp.int32)[None, :]
    quarter = jnp.sum(jnp.where(gamma_pick, phases[None, :], 0), axis=1)
    cosine = (quarter == 0).astype(jnp.float32) - (quarter == 2).astype(jnp.float32)
    sine_part = (quarter == 1).astype(jnp.float32) - (quarter == 3).astype(jnp.float32)
    return jnp.stack(
        [
            cosine * chosen_real - sine_part * chosen_imag,
            sine_part * chosen_real + cosine * chosen_imag,
        ]
    )


def local(tau_cols, elementals, need_ids, diagrams, phases, block_sizes):
    groups = lax.axis_size("snk")
    column = lax.axis_index("snk")
    full_width = tau_cols.shape[4]
    col_count = tau_cols.shape[3]
    sink_count = tau_cols.shape[2]
    diagram_rows = diagrams[0]
    starts = jnp.cumsum(block_sizes) - block_sizes
    offsets = jnp.arange(MAXB, dtype=jnp.int32)
    picked = jnp.take(elementals, need_ids, axis=2)
    arrived = lax.all_to_all(picked, "src", split_axis=2, concat_axis=0, tiled=True)
    gathered = arrived.reshape(full_width, 2, need_ids.shape[1], full_width)
    local_tau = tau_cols[:, 0]
    per_group = sink_count // groups
    half_turn = groups // 2
    packed = local_tau.reshape(2, groups, per_group, col_count, full_width)
    packed = jnp.roll(packed, -half_turn, axis=1)
    arrived_tau = lax.all_to_all(packed, "snk", split_axis=1, concat_axis=3, tiled=True)
    blocks = arrived_tau.reshape(2, per_group, full_width, full_width)
    results = jnp.stack(
        [
            slot_values(gathered, blocks[:, place], diagram_rows, phases)
            for place in range(per_group)
        ]
    )
    all_values = lax.all_gather(results, "snk", axis=0, tiled=True)
    all_values = jnp.roll(all_values, half_turn * per_group, axis=0)
    own_start = lax.dynamic_index_in_dim(starts, column, keepdims=False)
    own_size = lax.dynamic_index_in_dim(block_sizes, column, keepdims=False)
    own_filled = offsets < own_size
    own_times = jnp.where(own_filled, own_start + offsets, 0)
    correlators = jnp.take(all_values, own_times, axis=0) * own_filled[:, None, None].astype(
        jnp.float32
    )
    return correlators.reshape(1, 1, MAXB, 2, diagram_rows.shape[0])


def solution(mesh):
    placed = (
        P(None, "src", None, "snk", None),
        P("src", None, None, None),
        P(),
        P("src", None, None),
        P(),
        P(),
    )
    return jax.shard_map(
        local,
        mesh=mesh,
        in_specs=placed,
        out_specs=P("src", "snk", None, None, None),
        check_vma=False,
    )
```

profile of v0, /device:TPU:0, one launch (start us, length us, event | category | flops | bytes accessed | tf_op | source)
XLA Modules:
  0.0 94.8 jit_solution(11811888920916635707)
XLA Ops:
  0.0 1.1 %fusion.38 = (bf16[2,2,2,64,256]{4,3,2,1,0:T(8,128)(2,1)S(1)}, bf16[2,2,2,64,256]{4,3,2,1,0:T(8,128)(2,1)S(1)}) fusion(bf16[2,4,2,64,256]{4,3,2,1,0:T(8,128)(2,1)} %bitcast.147), kind=kLoop, calls=%fused_computation.106 | loop fusion | bytes 1048576 | tf_op jit(solution)/shard_map/jit(_roll_static)/slice | solution.py:72
  1.1 0.9 copy.35
  2.0 4.2 %all-to-all-start.1 = ((bf16[2,4,2,64,256]{4,3,2,0,1:T(8,128)(2,1)}), bf16[2,4,2,64,256]{4,3,2,0,1:T(8,128)(2,1)S(1)}, u32[]{:S(2)}, u32[]{:S(2)}) async-start(bf16[2,4,2,64,256]{4,3,2,0,1:T(8,128)(2,1)} %copy.35), calls=%async_computation.1 | async-start | bytes 1048576 | tf_op jit(solution)/shard_map/all_to_all | solution.py:73
  6.4 6.2 %gather_fusion = bf16[64,32,2,256]{3,0,2,1:T(8,128)(2,1)S(1)} fusion(bf16[32,2,256,256]{3,2,1,0:T(8,128)(2,1)} %param.7, s32[1024]{0:T(1024)S(1)} %pad_clamp_fusion.1), kind=kCustom, calls=%fused_computation | custom fusion | bytes 4194560 | tf_op jit(solution)/shard_map/jit(_take)/gather | solution.py:65
  12.5 2.1 %fusion = bf16[32,2,8,8,256]{4,3,1,0,2:T(8,128)(2,1)} fusion(pred[8,8]{1,0:T(8,128)(4,1)S(1)} %compare_and_fusion, bf16[64,32,2,256]{3,0,2,1:T(8,128)(2,1)S(1)} %gather_fusion), kind=kLoop, calls=%fused_computation.7 | loop fusion | flops 1048576 | bytes 4194368 | tf_op jit(solution)/shard_map/jit(_take)/select_n | solution.py:65
  15.1 6.5 %all-to-all-start = ((bf16[32,2,8,8,256]{4,3,1,0,2:T(8,128)(2,1)}), bf16[32,2,8,8,256]{4,3,1,0,2:T(8,128)(2,1)S(1)}, u32[]{:S(2)}, u32[]{:S(2)}) async-start(bf16[32,2,8,8,256]{4,3,1,0,2:T(8,128)(2,1)} %fusion), calls=%async_computation | async-start | bytes 4194304 | tf_op jit(solution)/shard_map/all_to_all | solution.py:66
  21.8 0.6 dynamic_slice.7
  22.4 0.6 dynamic_slice.8
  23.0 1.3 %fusion.32 = s32[3]{0:T(128)S(1)} fusion(s32[]{:T(128)} %bitcast.3, s32[]{:T(128)} %bitcast), kind=kLoop, calls=%fused_computation.97 | loop fusion | flops 18 | bytes 20 | tf_op jit(solution)/shard_map/jit(_take)/jit(_where)/select_n | solution.py:87
  24.3 1.3 %compare_and_fusion.1 = (pred[3]{0:T(512)(128)(4,1)S(1)}, f32[3]{0:T(128)S(1)}) fusion(s32[]{:T(128)} %bitcast.3, s32[]{:T(128)} %bitcast), kind=kLoop, calls=%fused_computation.85 | loop fusion | flops 30 | bytes 23 | tf_op jit(solution)/shard_map/jit(_take)/and | solution.py:87
  25.9 1.3 %fusion.17 = (bf16[1,2,256,256]{3,2,0,1:T(8,128)(2,1)S(1)}, bf16[1,2,256,256]{3,2,1,0:T(8,128)(2,1)}, bf16[1,2,256,256]{3,2,1,0:T(8,128)(2,1)}, bf16[1,2,256,256...) fusion(bf16[1,256,256]{2,1,0:T(8,128)(2,1)S(1)} %get-tuple-elem, ...), kind=kLoop, calls=%fused_computation.41 | loop fusion | flops 1048576 | bytes 2883584 | tf_op jit(solution)/shard_map/stack | solution.py:13
  27.2 43.1 %all-to-all-done = bf16[32,2,8,8,256]{4,3,1,0,2:T(8,128)(2,1)S(1)} async-done(((bf16[32,2,8,8,256]{4,3,1,0,2:T(8,128)(2,1)}), bf16[32,2,8,8,256]{4,3,1,0,2:T(8,128)(2,1)S(1)}, u32[]{:S(2)}, u32[]{:S(2)}) %all-to-all-start) | async-done | bytes 2097184 | tf_op jit(solution)/shard_map/all_to_all | solution.py:66
  70.2 0.7 fusion.37
  70.9 1.0 %copy-done = bf16[256,2,4,256]{3,2,1,0:T(4,128)(2,1)} copy-done((bf16[256,2,4,256]{3,2,1,0:T(4,128)(2,1)}, bf16[256,2,4,256]{3,2,1,0:T(4,128)(2,1)S(1)}, u32[]{:S(2)}) %copy-start) | copy-done | bytes 1048600
  71.9 0.7 bitcast_convert_fusion.2
  72.6 0.7 copy.41
  73.3 1.8 %fusion.1 = bf16[256,4,2,256,1]{3,0,2,1,4:T(8,128)(2,1)S(1)} fusion(bf16[256,2,4,256]{3,2,1,0:T(4,128)(2,1)S(1)} %get-tuple-element.9, bf16[1,2,256,256]{3,2,0,1:T(8,128)(2,1)} %get-tuple-element.48, bf16[1,2,256,256]{3,2,0,1:T(8,128)(2,1)} %get-tuple-element.51), kind=kOutput, calls=%fused_computation.8 | convolution fusion | flops 538443776 | bytes 2621440 | tf_op jit(solution)/shard_map/dot_general | solution.py:15
  75.1 4.9 %convolution_bitcast_fusion.1 = f32[4,2,4,2]{2,0,3,1:T(4,128)S(1)} fusion(bf16[256,4,2,256]{0,1,3,2:T(4,128)(2,1)S(1)} %copy.41, bf16[256,4,2,256,1]{3,0,2,1,4:T(8,128)(2,1)S(1)} %fusion.1), kind=kOutput, calls=%fused_computation.11 | convolution fusion | flops 8388608 | bytes 2097408 | tf_op jit(solution)/shard_map/dot_general | solution.py:27
  80.1 0.7 bitcast_convert_fusion
  80.8 0.7 copy.45
  81.5 1.7 %fusion.2 = bf16[256,4,2,256,1]{3,0,2,1,4:T(8,128)(2,1)S(1)} fusion(bf16[256,2,4,256]{3,2,1,0:T(4,128)(2,1)S(1)} %get-tuple-element.9, bf16[1,2,256,256]{3,2,0,1:T(8,128)(2,1)} %get-tuple-element.28, bf16[1,2,256,256]{3,2,0,1:T(8,128)(2,1)S(1)} %get-tuple-element.19), kind=kOutput, calls=%fused_computation.9 | convolution fusion | flops 538443776 | bytes 2621440 | tf_op jit(solution)/shard_map/dot_general | solution.py:15
  83.2 4.9 %convolution_bitcast_fusion = f32[4,2,4,2]{2,0,3,1:T(4,128)S(1)} fusion(bf16[256,4,2,256]{0,1,3,2:T(4,128)(2,1)S(1)} %copy.45, bf16[256,4,2,256,1]{3,0,2,1,4:T(8,128)(2,1)S(1)} %fusion.2), kind=kOutput, calls=%fused_computation.10 | convolution fusion | flops 8388608 | bytes 2097408 | tf_op jit(solution)/shard_map/dot_general | solution.py:27
  88.4 5.2 %all_gather.3 = f32[8,2,8]{2,1,0:T(2,128)S(1)} all-gather(f32[2,2,8]{2,1,0:T(2,128)S(1)} %pad_maximum_fusion.12), channel_id=1, replica_groups=mesh['src'=8,'snk'=4] {'snk'}, dimensions={0}, use_global_device_ids=true | all-gather | bytes 640 | tf_op jit(solution)/shard_map/all_gather | solution.py:81
  94.1 0.7 fusion.23
  (45 shorter events, 1.8 us)
Async XLA Ops:
  0.0 6.2 %copy-start.6 = (s32[8,8]{1,0:T(8,128)S(1)}, s32[8,8]{1,0:T(8,128)}, u32[]{:S(2)}) copy-start(s32[8,8]{1,0:T(8,128)} %param.8) | copy-start | bytes 772
  2.0 13.1 %all-to-all-start.1 = ((bf16[2,4,2,64,256]{4,3,2,0,1:T(8,128)(2,1)}), bf16[2,4,2,64,256]{4,3,2,0,1:T(8,128)(2,1)S(1)}, u32[]{:S(2)}, u32[]{:S(2)}) async-start(bf16[2,4,2,64,256]{4,3,2,0,1:T(8,128)(2,1)} %copy.35), calls=%async_computation.1 | async-start | bytes 1048576 | tf_op jit(solution)/shard_map/all_to_all | solution.py:73
  14.7 6.9 %copy-start.7 = (s32[1,8,3]{1,0,2:T(1,128)S(1)}, s32[1,8,3]{1,0,2:T(1,128)}, u32[]{:S(2)}) copy-start(s32[1,8,3]{1,0,2:T(1,128)} %param.9) | copy-start | bytes 292
  14.7 6.9 %copy-start.8 = (s32[4]{0:T(128)S(1)}, s32[4]{0:T(128)}, u32[]{:S(2)}) copy-start(s32[4]{0:T(128)} %param.11) | copy-start | bytes 52
  14.7 10.9 %copy-start.9 = (s32[16]{0:T(128)S(1)}, s32[16]{0:T(128)}, u32[]{:S(2)}) copy-start(s32[16]{0:T(128)} %param.10) | copy-start | bytes 196
  15.1 55.2 %all-to-all-start = ((bf16[32,2,8,8,256]{4,3,1,0,2:T(8,128)(2,1)}), bf16[32,2,8,8,256]{4,3,1,0,2:T(8,128)(2,1)S(1)}, u32[]{:S(2)}, u32[]{:S(2)}) async-start(bf16[32,2,8,8,256]{4,3,1,0,2:T(8,128)(2,1)} %fusion), calls=%async_computation | async-start | bytes 4194304 | tf_op jit(solution)/shard_map/all_to_all | solution.py:66
  70.2 1.7 %copy-start.4 = (bf16[1,2,256,256]{3,2,1,0:T(8,128)(2,1)S(1)}, bf16[1,2,256,256]{3,2,1,0:T(8,128)(2,1)}, u32[]{:S(2)}) copy-start(bf16[1,2,256,256]{3,2,1,0:T(8,128)(2,1)} %get-tuple-element.49) | copy-start | bytes 786436
  70.2 1.7 %copy-start.5 = (bf16[1,2,256,256]{3,2,1,0:T(8,128)(2,1)S(1)}, bf16[1,2,256,256]{3,2,1,0:T(8,128)(2,1)}, u32[]{:S(2)}) copy-start(bf16[1,2,256,256]{3,2,1,0:T(8,128)(2,1)} %get-tuple-element.50) | copy-start | bytes 786436
  70.9 1.0 %copy-start = (bf16[256,2,4,256]{3,2,1,0:T(4,128)(2,1)}, bf16[256,2,4,256]{3,2,1,0:T(4,128)(2,1)S(1)}, u32[]{:S(2)}) copy-start(bf16[256,2,4,256]{3,2,1,0:T(4,128)(2,1)S(1)} %get-tuple-element.10) | copy-start | bytes 3145732
  75.1 5.0 %copy-start.1 = (bf16[256,2,4,256]{3,2,1,0:T(4,128)(2,1)S(1)}, bf16[256,2,4,256]{3,2,1,0:T(4,128)(2,1)}, u32[]{:S(2)}) copy-start(bf16[256,2,4,256]{3,2,1,0:T(4,128)(2,1)} %copy-done) | copy-start | bytes 3145732
  75.1 5.0 %copy-start.2 = (bf16[1,2,256,256]{3,2,1,0:T(8,128)(2,1)S(1)}, bf16[1,2,256,256]{3,2,1,0:T(8,128)(2,1)}, u32[]{:S(2)}) copy-start(bf16[1,2,256,256]{3,2,1,0:T(8,128)(2,1)} %get-tuple-element.20) | copy-start | bytes 786436
  75.1 5.0 %copy-start.3 = (bf16[1,2,256,256]{3,2,1,0:T(8,128)(2,1)S(1)}, bf16[1,2,256,256]{3,2,1,0:T(8,128)(2,1)}, u32[]{:S(2)}) copy-start(bf16[1,2,256,256]{3,2,1,0:T(8,128)(2,1)} %get-tuple-element.27) | copy-start | bytes 786436
where the time goes:
time: 95.2 us; the launch traced here: 94.8 us
  waiting for transfers between devices  43.5 us (46%)
  matrix products  14.7 us (15%)
  local copies, waits for them, and re-layouts  13.2 us (14%)
  starting transfers between devices  10.8 us (11%)
  other arithmetic  7.21 us (8%)
  blocking collectives  5.19 us (5%)
    all_to_all x1, waiting for transfers between devices, local(): lax.all_to_all(picked, 'src', split_axis=2, concat_axis=0, tiled=True)  43.1 us
    dot_general x2, matrix products, slot_values(): lax.dot_general(left_node, right_node, (((0, 3), (3, 0)), ((), ())), pref...  9.84 us
    all_to_all x1, starting transfers between devices, local(): lax.all_to_all(picked, 'src', split_axis=2, concat_axis=0, tiled=True)  6.52 us
    gather x1, local copies, waits for them, and re-layouts, local(): picked = jnp.take(elementals, need_ids, axis=2)  6.18 us
    all_gather x1, blocking collectives, local(): all_values = lax.all_gather(results, 'snk', axis=0, tiled=True)  5.19 us
    all_to_all x1, starting transfers between devices, local(): lax.all_to_all(packed, 'snk', split_axis=1, concat_axis=3, tiled=True)  4.24 us
    dot_general x2, matrix products, slot_values(): lax.dot_general(gathered[:, :, :NSN], left_stack, (((1, 3), (0, 3)), ((),...  3.47 us
    select_n x2, other arithmetic, local(): picked = jnp.take(elementals, need_ids, axis=2)  2.12 us
  transfers between devices with their start and end apart: 2, of which 2 were waited for; matrix products, arithmetic and copies ran while one was open for 15% of the time, Pallas kernels for 0%

commit v1 on v0

--- a/solution.py
+++ b/solution.py
@@ -63,7 +63,10 @@
     starts = jnp.cumsum(block_sizes) - block_sizes
     offsets = jnp.arange(MAXB, dtype=jnp.int32)
     picked = jnp.take(elementals, need_ids, axis=2)
-    arrived = lax.all_to_all(picked, "src", split_axis=2, concat_axis=0, tiled=True)
+    arrived = jnp.concatenate(
+        lax.all_to_all(jnp.stack(jnp.split(picked, lax.axis_size("src"), axis=2)), "src", 0, 0),
+        axis=0,
+    )
     gathered = arrived.reshape(full_width, 2, need_ids.shape[1], full_width)
     local_tau = tau_cols[:, 0]
     per_group = sink_count // groups

time: 95.2 us -> 103 us (1.082)
  local copies, waits for them, and re-layouts: 13.2 us -> 16.6 us
  waiting for transfers between devices: 43.5 us -> 46.2 us
  matrix products: 14.7 us -> 16.7 us
  other arithmetic: 7.21 us -> 6.14 us
    all_to_all x1, waiting for transfers between devices: 43.1 us -> 46.2 us  [local(): lax.all_to_all(jnp.stack(jnp.split(picked, lax.axis_size('src'), axis=2))...]
    convert_element_type x2, local copies, waits for them, and re-layouts: 1.42 us -> 3.49 us  [slot_values(): right_node = lax.dot_general(gathered[:, :, NSN:], right_stack, (((1, 3),...]
    dot_general x2, matrix products: 1.42 us -> 3.38 us  [slot_values(): lax.dot_general(gathered[:, :, NSN:], right_stack, (((1, 3), (0, 2)), (()...]
    unnamed x21 -> x26, local copies, waits for them, and re-layouts: 0.99 us -> 2.91 us
  transfers between devices with their start and end apart: 2 -> 2, of which waited for: 2 -> 1; matrix products, arithmetic and copies ran while one was open for 15% -> 13% of each run, Pallas kernels for 0% -> 0%
where the time goes in v1:
time: 103 us; the launch traced here: 102 us
  waiting for transfers between devices  46.2 us (45%)
  matrix products  16.7 us (16%)
  local copies, waits for them, and re-layouts  16.6 us (16%)
  starting transfers between devices  10.9 us (11%)
  other arithmetic  6.14 us (6%)
  blocking collectives  5.19 us (5%)
    all_to_all x1, waiting for transfers between devices, local(): lax.all_to_all(jnp.stack(jnp.split(picked, lax.axis_size('src'), axis=2))...  46.2 us
    dot_general x2, matrix products, slot_values(): lax.dot_general(left_node, right_node, (((0, 3), (3, 0)), ((), ())), pref...  9.85 us
    all_to_all x1, starting transfers between devices, local(): lax.all_to_all(jnp.stack(jnp.split(picked, lax.axis_size('src'), axis=2))...  6.7 us
    gather x1, local copies, waits for them, and re-layouts, local(): picked = jnp.take(elementals, need_ids, axis=2)  6.18 us
    all_gather x1, blocking collectives, local(): all_values = lax.all_gather(results, 'snk', axis=0, tiled=True)  5.19 us
    all_to_all x1, starting transfers between devices, local(): lax.all_to_all(packed, 'snk', split_axis=1, concat_axis=3, tiled=True)  4.24 us
    convert_element_type x2, local copies, waits for them, and re-layouts, slot_values(): right_node = lax.dot_general(gathered[:, :, NSN:], right_stack, (((1, 3),...  3.49 us
    dot_general x2, matrix products, slot_values(): lax.dot_general(gathered[:, :, :NSN], left_stack, (((1, 3), (0, 3)), ((),...  3.45 us
  transfers between devices with their start and end apart: 2, of which 1 were waited for; matrix products, arithmetic and copies ran while one was open for 13% of the time, Pallas kernels for 0%

profile of v1, /device:TPU:0, one launch (start us, length us, event | category | flops | bytes accessed | tf_op | source)
XLA Modules:
  0.0 102.1 jit_solution(13366572188466838303)
XLA Ops:
  0.0 1.1 %fusion.45 = (bf16[2,2,2,64,256]{4,3,2,1,0:T(8,128)(2,1)S(1)}, bf16[2,2,2,64,256]{4,3,2,1,0:T(8,128)(2,1)S(1)}) fusion(bf16[2,4,2,64,256]{4,3,2,1,0:T(8,128)(2,1)} %bitcast.177), kind=kLoop, calls=%fused_computation.121 | loop fusion | bytes 1048576 | tf_op jit(solution)/shard_map/jit(_roll_static)/slice | solution.py:75
  1.2 0.9 copy.52
  2.0 4.2 %all-to-all-start.1 = ((bf16[2,4,2,64,256]{4,3,2,0,1:T(8,128)(2,1)}), bf16[2,4,2,64,256]{4,3,2,0,1:T(8,128)(2,1)S(1)}, u32[]{:S(2)}, u32[]{:S(2)}) async-start(bf16[2,4,2,64,256]{4,3,2,0,1:T(8,128)(2,1)} %copy.52), calls=%async_computation.1 | async-start | bytes 1048576 | tf_op jit(solution)/shard_map/all_to_all | solution.py:76
  6.5 0.6 dynamic_slice.7
  7.1 0.6 dynamic_slice.8
  7.7 1.2 %fusion.40 = s32[3]{0:T(128)S(1)} fusion(s32[]{:T(128)} %bitcast.3, s32[]{:T(128)} %bitcast), kind=kLoop, calls=%fused_computation.113 | loop fusion | flops 18 | bytes 20 | tf_op jit(solution)/shard_map/jit(_take)/jit(_where)/select_n | solution.py:90
  9.0 6.2 %gather_fusion = bf16[64,32,2,256]{3,0,2,1:T(8,128)(2,1)S(1)} fusion(bf16[32,2,256,256]{3,2,1,0:T(8,128)(2,1)} %param.7, s32[1024]{0:T(1024)S(1)} %get-tuple-element.47), kind=kCustom, calls=%fused_computation | custom fusion | bytes 4194560 | tf_op jit(solution)/shard_map/jit(_take)/gather | solution.py:65
  15.2 1.3 %fusion = bf16[32,2,8,8,256]{4,0,1,3,2:T(8,128)(2,1)S(1)} fusion(bf16[8,8,32,2,256]{4,1,0,3,2:T(8,128)(2,1)S(1)} %bitcast.170, pred[8,8]{1,0:T(8,128)(4,1)S(1)} %compare_and_fusion), kind=kLoop, calls=%fused_computation.7 | loop fusion | flops 1048576 | bytes 4194368 | tf_op jit(solution)/shard_map/jit(_take)/select_n | solution.py:65
  16.7 1.3 %copy-done = bf16[8,32,2,1,8,256]{5,1,2,4,3,0:T(8,128)(2,1)} copy-done((bf16[8,32,2,1,8,256]{5,1,2,4,3,0:T(8,128)(2,1)}, bf16[8,32,2,1,8,256]{5,1,2,4,3,0:T(8,128)(2,1)S(1)}, u32[]{:S(2)}) %copy-start) | copy-done | bytes 2097176
  18.0 6.7 %all-to-all-start = ((bf16[8,32,2,1,8,256]{5,1,2,4,3,0:T(8,128)(2,1)}), bf16[8,32,2,1,8,256]{5,1,2,4,3,0:T(8,128)(2,1)S(1)}, u32[]{:S(2)}, u32[]{:S(2)}) async-start(bf16[8,32,2,1,8,256]{5,1,2,4,3,0:T(8,128)(2,1)} %copy-done), calls=%async_computation | async-start | bytes 4194304 | tf_op jit(solution)/shard_map/all_to_all | solution.py:67
  24.7 1.2 %compare_and_fusion.1 = (pred[3]{0:T(512)(128)(4,1)S(1)}, f32[3]{0:T(128)S(1)}) fusion(s32[]{:T(128)} %bitcast.3, s32[]{:T(128)} %bitcast), kind=kLoop, calls=%fused_computation.101 | loop fusion | flops 30 | bytes 23 | tf_op jit(solution)/shard_map/jit(_take)/and | solution.py:90
  26.3 1.1 %fusion.17 = (bf16[1,2,256,256]{3,2,0,1:T(8,128)(2,1)}, bf16[1,2,256,256]{3,2,1,0:T(8,128)(2,1)S(1)}, bf16[1,2,256,256]{3,2,1,0:T(8,128)(2,1)S(1)}, bf16[1,2,256...) fusion(bf16[1,256,256]{2,1,0:T(8,128)(2,1)S(1)} %get-tuple-elem, ...), kind=kLoop, calls=%fused_computation.41 | loop fusion | flops 1048576 | bytes 2883584 | tf_op jit(solution)/shard_map/stack | solution.py:13
  27.4 46.2 %all-to-all-done = bf16[8,32,2,1,8,256]{5,1,2,4,3,0:T(8,128)(2,1)S(1)} async-done(((bf16[8,32,2,1,8,256]{5,1,2,4,3,0:T(8,128)(2,1)}), bf16[8,32,2,1,8,256]{5,1,2,4,3,0:T(8,128)(2,1)S(1)}, u32[]{:S(2)}, u32[]{:S(2)}) %all-to-all-start) | async-done | bytes 2097184 | tf_op jit(solution)/shard_map/all_to_all | solution.py:67
  73.8 1.3 %copy-done.1 = bf16[8,32,2,1,8,256]{5,1,0,2,4,3:T(8,128)(2,1)} copy-done((bf16[8,32,2,1,8,256]{5,1,0,2,4,3:T(8,128)(2,1)}, bf16[8,32,2,1,8,256]{5,1,0,2,4,3:T(8,128)(2,1)S(1)}, u32[]{:S(2)}) %copy-start.1) | copy-done | bytes 2097176
  75.1 1.7 %bitcast_convert_fusion = bf16[256,4,2,256]{3,0,2,1:T(8,128)(2,1)} fusion(bf16[256,2,8,256]{3,0,1,2:T(8,128)(2,1)S(1)} %bitcast.173, bf16[1,2,256,256]{3,2,1,0:T(8,128)(2,1)S(1)} %get-tuple-element.18, bf16[1,2,256,256]{3,2,1,0:T(8,128)(2,1)S(1)} %get-tuple-element.25), kind=kOutput, calls=%fused_computation.2 | convolution fusion | flops 537657344 | bytes 2621440 | tf_op jit(solution)/shard_map/dot_general | solution.py:21
  76.8 1.8 %copy.61 = bf16[256,4,2,256]{0,1,3,2:T(4,128)(2,1)S(1)} copy(bf16[256,4,2,256]{3,0,2,1:T(8,128)(2,1)} %bitcast_convert_fusion) | data formatting | bytes 2097152 | tf_op jit(solution)/shard_map/convert_element_type | solution.py:26
  78.7 1.8 %fusion.2 = bf16[256,4,2,256,1]{3,0,2,1,4:T(8,128)(2,1)S(1)} fusion(bf16[256,2,8,256]{3,0,1,2:T(8,128)(2,1)S(1)} %bitcast.174, bf16[1,2,256,256]{3,2,0,1:T(8,128)(2,1)} %get-tuple-element.26, bf16[1,2,256,256]{3,2,0,1:T(8,128)(2,1)} %get-tuple-element.17), kind=kOutput, calls=%fused_computation.9 | convolution fusion | flops 538443776 | bytes 2621440 | tf_op jit(solution)/shard_map/dot_general | solution.py:15
  80.5 4.9 %convolution_bitcast_fusion = f32[4,2,4,2]{2,0,3,1:T(4,128)S(1)} fusion(bf16[256,4,2,256]{0,1,3,2:T(4,128)(2,1)S(1)} %copy.61, bf16[256,4,2,256,1]{3,0,2,1,4:T(8,128)(2,1)S(1)} %fusion.2), kind=kOutput, calls=%fused_computation.10 | convolution fusion | flops 8388608 | bytes 2097408 | tf_op jit(solution)/shard_map/dot_general | solution.py:27
  85.5 1.7 %bitcast_convert_fusion.2 = bf16[256,4,2,256]{3,0,2,1:T(8,128)(2,1)} fusion(bf16[256,2,8,256]{3,0,1,2:T(8,128)(2,1)S(1)} %bitcast.175, bf16[1,2,256,256]{3,2,1,0:T(8,128)(2,1)S(1)} %copy-done.4, bf16[1,2,256,256]{3,2,1,0:T(8,128)(2,1)S(1)} %copy-done.3), kind=kOutput, calls=%fused_computation.4 | convolution fusion | flops 537657344 | bytes 2621440 | tf_op jit(solution)/shard_map/dot_general | solution.py:21
  87.2 1.7 %copy.57 = bf16[256,4,2,256]{0,1,3,2:T(4,128)(2,1)S(1)} copy(bf16[256,4,2,256]{3,0,2,1:T(8,128)(2,1)} %bitcast_convert_fusion.2) | data formatting | bytes 2097152 | tf_op jit(solution)/shard_map/convert_element_type | solution.py:26
  88.8 1.7 %fusion.1 = bf16[256,4,2,256,1]{3,0,2,1,4:T(8,128)(2,1)S(1)} fusion(bf16[256,2,8,256]{3,0,1,2:T(8,128)(2,1)S(1)} %bitcast.176, bf16[1,2,256,256]{3,2,0,1:T(8,128)(2,1)S(1)} %get-tuple-element.48, bf16[1,2,256,256]{3,2,0,1:T(8,128)(2,1)} %get-tuple-element.51), kind=kOutput, calls=%fused_computation.8 | convolution fusion | flops 538443776 | bytes 2621440 | tf_op jit(solution)/shard_map/dot_general | solution.py:15
  90.5 4.9 %convolution_bitcast_fusion.1 = f32[4,2,4,2]{2,0,3,1:T(4,128)S(1)} fusion(bf16[256,4,2,256]{0,1,3,2:T(4,128)(2,1)S(1)} %copy.57, bf16[256,4,2,256,1]{3,0,2,1,4:T(8,128)(2,1)S(1)} %fusion.1), kind=kOutput, calls=%fused_computation.11 | convolution fusion | flops 8388608 | bytes 2097408 | tf_op jit(solution)/shard_map/dot_general | solution.py:27
  95.6 5.2 %all_gather.3 = f32[8,2,8]{2,1,0:T(2,128)S(1)} all-gather(f32[2,2,8]{2,1,0:T(2,128)S(1)} %pad_maximum_fusion.12), channel_id=1, replica_groups=mesh['src'=8,'snk'=4] {'snk'}, dimensions={0}, use_global_device_ids=true | all-gather | bytes 640 | tf_op jit(solution)/shard_map/all_gather | solution.py:84
  101.4 0.7 fusion.31
  (50 shorter events, 1.8 us)
Async XLA Ops:
  0.0 6.3 %copy-start.5 = (s32[8,8]{1,0:T(8,128)S(1)}, s32[8,8]{1,0:T(8,128)}, u32[]{:S(2)}) copy-start(s32[8,8]{1,0:T(8,128)} %param.8) | copy-start | bytes 772
  0.0 6.3 %copy-start.7 = (s32[4]{0:T(128)S(1)}, s32[4]{0:T(128)}, u32[]{:S(2)}) copy-start(s32[4]{0:T(128)} %param.11) | copy-start | bytes 52
  2.0 16.0 %all-to-all-start.1 = ((bf16[2,4,2,64,256]{4,3,2,0,1:T(8,128)(2,1)}), bf16[2,4,2,64,256]{4,3,2,0,1:T(8,128)(2,1)S(1)}, u32[]{:S(2)}, u32[]{:S(2)}) async-start(bf16[2,4,2,64,256]{4,3,2,0,1:T(8,128)(2,1)} %copy.52), calls=%async_computation.1 | async-start | bytes 1048576 | tf_op jit(solution)/shard_map/all_to_all | solution.py:76
  16.7 1.3 %copy-start = (bf16[8,32,2,1,8,256]{5,1,2,4,3,0:T(8,128)(2,1)}, bf16[8,32,2,1,8,256]{5,1,2,4,3,0:T(8,128)(2,1)S(1)}, u32[]{:S(2)}) copy-start(bf16[8,32,2,1,8,256]{5,1,2,4,3,0:T(8,128)(2,1)S(1)} %fusion.23) | copy-start | bytes 6291460
  18.0 6.7 %copy-start.6 = (s32[1,8,3]{1,0,2:T(1,128)S(1)}, s32[1,8,3]{1,0,2:T(1,128)}, u32[]{:S(2)}) copy-start(s32[1,8,3]{1,0,2:T(1,128)} %param.9) | copy-start | bytes 292
  18.0 8.0 %copy-start.8 = (s32[16]{0:T(128)S(1)}, s32[16]{0:T(128)}, u32[]{:S(2)}) copy-start(s32[16]{0:T(128)} %param.10) | copy-start | bytes 196
  18.0 55.5 %all-to-all-start = ((bf16[8,32,2,1,8,256]{5,1,2,4,3,0:T(8,128)(2,1)}), bf16[8,32,2,1,8,256]{5,1,2,4,3,0:T(8,128)(2,1)S(1)}, u32[]{:S(2)}, u32[]{:S(2)}) async-start(bf16[8,32,2,1,8,256]{5,1,2,4,3,0:T(8,128)(2,1)} %copy-done), calls=%async_computation | async-start | bytes 4194304 | tf_op jit(solution)/shard_map/all_to_all | solution.py:67
  73.8 1.3 %copy-start.1 = (bf16[8,32,2,1,8,256]{5,1,0,2,4,3:T(8,128)(2,1)}, bf16[8,32,2,1,8,256]{5,1,0,2,4,3:T(8,128)(2,1)S(1)}, u32[]{:S(2)}) copy-start(bf16[8,32,2,1,8,256]{5,1,0,2,4,3:T(8,128)(2,1)S(1)} %copy.51) | copy-start | bytes 6291460
  76.8 1.9 %copy-start.2 = (bf16[8,32,2,1,8,256]{5,1,0,2,4,3:T(8,128)(2,1)S(1)}, bf16[8,32,2,1,8,256]{5,1,0,2,4,3:T(8,128)(2,1)}, u32[]{:S(2)}) copy-start(bf16[8,32,2,1,8,256]{5,1,0,2,4,3:T(8,128)(2,1)} %copy-done.1) | copy-start | bytes 6291460
  80.5 5.0 %copy-start.3 = (bf16[1,2,256,256]{3,2,1,0:T(8,128)(2,1)S(1)}, bf16[1,2,256,256]{3,2,1,0:T(8,128)(2,1)}, u32[]{:S(2)}) copy-start(bf16[1,2,256,256]{3,2,1,0:T(8,128)(2,1)} %get-tuple-element.49) | copy-start | bytes 786436
  80.5 5.0 %copy-start.4 = (bf16[1,2,256,256]{3,2,1,0:T(8,128)(2,1)S(1)}, bf16[1,2,256,256]{3,2,1,0:T(8,128)(2,1)}, u32[]{:S(2)}) copy-start(bf16[1,2,256,256]{3,2,1,0:T(8,128)(2,1)} %get-tuple-element.50) | copy-start | bytes 786436
